TPU v7x, 32 devices: a whole 2x2x4 slice. The times are simulated.
32 devices in a mesh: dp: 8 (over z, x), mp: 4 (over y, core).
Axes of the slice: x: 2, y: 2, z: 4, core: 2. Of those that a mesh axis runs over, the one named last changes fastest.
Arguments:
- tokens: bfloat16 [32768, 1024], P('dp'), may hold values from -12 to 12
- out_grad: bfloat16 [32768, 1024], P('dp'), may hold values from -12 to 12
- qk_weight: float32 [2, 1024, 256], P(None, 'dp'), may hold values from -0.1875 to 0.1875
- qk_first: float32 [2, 1024, 256], P(None, 'dp'), may hold values from -0.0048828125 to 0.0048828125
- qk_second: float32 [2, 1024, 256], P(None, 'dp'), may hold values from 5.839972e-07 to 2.3359887e-06
- qk_average: float32 [2, 1024, 256], P(None, 'dp'), may hold values from -0.1875 to 0.1875
- value_weight: float32 [1024, 1024], P('dp', 'mp'), may hold values from -0.1875 to 0.1875
- value_first: float32 [1024, 1024], P('dp', 'mp'), may hold values from -0.0024414062 to 0.0024414062
- value_second: float32 [1024, 1024], P('dp', 'mp'), may hold values from 1.9069296e-07 to 7.6277183e-07
- value_average: float32 [1024, 1024], P('dp', 'mp'), may hold values from -0.1875 to 0.1875
- output_weight: float32 [1024, 1024], P('mp', 'dp'), may hold values from -1.5 to 1.5
- output_first: float32 [1024, 1024], P('mp', 'dp'), may hold values from -0.00048828125 to 0.00048828125
- output_second: float32 [1024, 1024], P('mp', 'dp'), may hold values from 6.7040493e-09 to 2.6816197e-08
- output_average: float32 [1024, 1024], P('mp', 'dp'), may hold values from -1.5 to 1.5
- gate_up_weight: float32 [2, 1024, 2752], P(None, 'dp', 'mp'), may hold values from -0.1875 to 0.1875
- gate_up_first: float32 [2, 1024, 2752], P(None, 'dp', 'mp'), may hold values from -0.0009765625 to 0.0009765625
- gate_up_second: float32 [2, 1024, 2752], P(None, 'dp', 'mp'), may hold values from 3.2775354e-08 to 1.3110142e-07
- gate_up_average: float32 [2, 1024, 2752], P(None, 'dp', 'mp'), may hold values from -0.1875 to 0.1875
- down_weight: float32 [2752, 1024], P('mp', 'dp'), may hold values from -0.109375 to 0.109375
- down_first: float32 [2752, 1024], P('mp', 'dp'), may hold values from -0.001953125 to 0.001953125
- down_second: float32 [2752, 1024], P('mp', 'dp'), may hold values from 1.0726479e-07 to 4.2905916e-07
- down_average: float32 [2752, 1024], P('mp', 'dp'), may hold values from -0.109375 to 0.109375
- gains: float32 [2, 1024], P(None, 'dp'), may hold values from 0.5 to 1.5
- gains_first: float32 [2, 1024], P(None, 'dp'), may hold values from -0.0034179688 to 0.0034179688
- gains_second: float32 [2, 1024], P(None, 'dp'), may hold values from 2.9795777e-07 to 1.1918311e-06
- gains_average: float32 [2, 1024], P(None, 'dp'), may hold values from 0.5 to 1.5
Outputs:
- block_out: bfloat16 [32768, 1024], P('dp', 'mp')
- input_grad: float32 [32768, 1024], P('dp', 'mp')
- grad_norm: float32 [], replicated
- qk_first_new: float32 [2, 1024, 256], P(None, 'dp')
- qk_second_new: float32 [2, 1024, 256], P(None, 'dp')
- qk_new: float32 [2, 1024, 256], P(None, 'dp')
- qk_average_new: float32 [2, 1024, 256], P(None, 'dp')
- value_first_new: float32 [1024, 1024], P('dp', 'mp')
- value_second_new: float32 [1024, 1024], P('dp', 'mp')
- value_new: float32 [1024, 1024], P('dp', 'mp')
- value_average_new: float32 [1024, 1024], P('dp', 'mp')
- output_first_new: float32 [1024, 1024], P('mp', 'dp')
- output_second_new: float32 [1024, 1024], P('mp', 'dp')
- output_new: float32 [1024, 1024], P('mp', 'dp')
- output_average_new: float32 [1024, 1024], P('mp', 'dp')
- gate_up_first_new: float32 [2, 1024, 2752], P(None, 'dp', 'mp')
- gate_up_second_new: float32 [2, 1024, 2752], P(None, 'dp', 'mp')
- gate_up_new: float32 [2, 1024, 2752], P(None, 'dp', 'mp')
- gate_up_average_new: float32 [2, 1024, 2752], P(None, 'dp', 'mp')
- down_first_new: float32 [2752, 1024], P('mp', 'dp')
- down_second_new: float32 [2752, 1024], P('mp', 'dp')
- down_new: float32 [2752, 1024], P('mp', 'dp')
- down_average_new: float32 [2752, 1024], P('mp', 'dp')
- gains_first_new: float32 [2, 1024], P(None, 'dp')
- gains_second_new: float32 [2, 1024], P(None, 'dp')
- gains_new: float32 [2, 1024], P(None, 'dp')
- gains_average_new: float32 [2, 1024], P(None, 'dp')
All inputs are finite; a program needn't handle non-finite values.
Results may differ from a plain program's by a relative error of at most 0.018.
Values may be sent and summed in bfloat16 or wider, within the bound.
A program may use at most 256 MiB of HBM per device.

v0:
```python
import math
import jax
import jax.numpy as jnp
from jax import lax
from jax.sharding import PartitionSpec as P

D = 1024
H = 16
F = 16
VH = 64
FF = 2752
V_ALL = 1024
LEN = 1024
STEP = 5


def inner(left, right):
    return lax.dot_general(
        left, right, (((0,), (0,)), ((), ())), preferred_element_type=jnp.float32
    )


def against(left, right):
    return lax.dot_general(
        left, right, (((1,), (1,)), ((), ())), preferred_element_type=jnp.float32
    )


def rms_scale(values):
    return lax.rsqrt(jnp.mean(values * values, axis=1, keepdims=True) + 1e-05)


def score_table(query, keys):
    length = query.shape[0]
    causal = (jnp.arange(length)[:, None] >= jnp.arange(length)[None, :]).astype(jnp.float32)
    tiled = jnp.einsum("ihf,jhf->hij", query, keys, preferred_element_type=jnp.float32) / math.sqrt(
        query.shape[2]
    )
    return (tiled, causal)


def mix_forward(parts):
    query, keys, values = parts
    tiled, causal = score_table(query, keys)
    kernel = causal * (1.0 + tiled + 0.5 * tiled * tiled)
    numer = jnp.einsum(
        "hij,jhv->ihv", kernel.astype(jnp.bfloat16), values, preferred_element_type=jnp.float32
    )
    return (numer, jnp.sum(kernel, axis=2).T)


def mix_backward(parts):
    query, keys, values, numer, denom, grad_mixed = parts
    tiled, causal = score_table(query, keys)
    kernel = causal * (1.0 + tiled + 0.5 * tiled * tiled)
    grad_numer = (grad_mixed / denom[:, :, None]).astype(jnp.bfloat16)
    grad_denom = -jnp.sum(grad_mixed * numer, axis=2) / (denom * denom)
    grad_kernel = (
        jnp.einsum("ihv,jhv->hij", grad_numer, values, preferred_element_type=jnp.float32)
        + grad_denom.T[:, :, None]
    )
    grad_tiled = (causal * grad_kernel * (1.0 + tiled)).astype(jnp.bfloat16)
    root = math.sqrt(query.shape[2])
    grad_values = jnp.einsum(
        "hij,ihv->jhv", kernel.astype(jnp.bfloat16), grad_numer, preferred_element_type=jnp.float32
    ).astype(jnp.bfloat16)
    grad_query = (
        jnp.einsum("hij,jhf->ihf", grad_tiled, keys, preferred_element_type=jnp.float32) / root
    ).astype(jnp.bfloat16)
    grad_keys = (
        jnp.einsum("hij,ihf->jhf", grad_tiled, query, preferred_element_type=jnp.float32) / root
    ).astype(jnp.bfloat16)
    return (grad_query, grad_keys, grad_values)


def adam_step(grad, first, second, weight, average, rate):
    first = 0.5 * first + 0.5 * grad
    second = 0.5 * second + 0.5 * grad * grad
    correct = 1.0 - 0.5**STEP
    weight = weight - rate * (first / correct / (jnp.sqrt(second / correct) + 1e-08) + 0.1 * weight)
    average = 0.5 * average + 0.5 * weight
    return (first, second, weight, average)


def on_device(
    tokens,
    out_grad,
    qk_weight,
    qk_first,
    qk_second,
    qk_average,
    value_weight,
    value_first,
    value_second,
    value_average,
    output_weight,
    output_first,
    output_second,
    output_average,
    gate_up_weight,
    gate_up_first,
    gate_up_second,
    gate_up_average,
    down_weight,
    down_first,
    down_second,
    down_average,
    gains,
    gains_first,
    gains_second,
    gains_average,
):
    groups = lax.axis_size("mp")
    rank = lax.axis_index("mp")
    qk_full, value_local, output_local, gate_up_local, down_local, gains_full = (
        lax.all_gather(qk_weight.astype(jnp.bfloat16), "dp", axis=1, tiled=True),
        lax.all_gather(value_weight.astype(jnp.bfloat16), "dp", axis=0, tiled=True),
        lax.all_gather(output_weight.astype(jnp.bfloat16), "dp", axis=1, tiled=True),
        lax.all_gather(gate_up_weight.astype(jnp.bfloat16), "dp", axis=1, tiled=True),
        lax.all_gather(down_weight.astype(jnp.bfloat16), "dp", axis=1, tiled=True),
        lax.all_gather(gains.astype(jnp.bfloat16), "dp", axis=1, tiled=True),
    )
    width = qk_full.shape[2] // groups
    qk_local = lax.dynamic_slice_in_dim(qk_full, rank * width, width, 2)
    tok_count = tokens.shape[0]
    seq_count = tok_count // LEN
    heads_here = H // groups
    cols = tokens.shape[1] // groups
    col_start = rank * cols
    first_gain = gains_full[0].astype(jnp.float32)
    second_gain = gains_full[1].astype(jnp.float32)
    inputs = tokens.astype(jnp.float32)
    scale_one = rms_scale(inputs)
    normed_one = inputs * scale_one
    hidden_one = (normed_one * first_gain).astype(jnp.bfloat16)
    query = jnp.dot(hidden_one, qk_local[0], preferred_element_type=jnp.float32).astype(
        jnp.bfloat16
    )
    keys = jnp.dot(hidden_one, qk_local[1], preferred_element_type=jnp.float32).astype(jnp.bfloat16)
    values = jnp.dot(hidden_one, value_local, preferred_element_type=jnp.float32).astype(
        jnp.bfloat16
    )
    head_query = query.reshape(seq_count, LEN, heads_here, F)
    head_keys = keys.reshape(seq_count, LEN, heads_here, F)
    head_values = values.reshape(seq_count, LEN, heads_here, VH)
    numer, denom = lax.map(mix_forward, (head_query, head_keys, head_values))
    mixed = (numer / denom[:, :, :, None]).astype(jnp.bfloat16).reshape(tok_count, heads_here * VH)
    attn_part = jnp.dot(mixed, output_local, preferred_element_type=jnp.float32)
    resid = inputs + lax.psum(attn_part.astype(jnp.bfloat16), "mp").astype(jnp.float32)
    scale_two = rms_scale(resid)
    normed_two = resid * scale_two
    hidden_two = (normed_two * second_gain).astype(jnp.bfloat16)
    gate = jnp.dot(hidden_two, gate_up_local[0], preferred_element_type=jnp.float32)
    lift = jnp.dot(hidden_two, gate_up_local[1], preferred_element_type=jnp.float32)
    sigma = jax.nn.sigmoid(gate)
    activ = (gate * sigma * lift).astype(jnp.bfloat16)
    down_part = jnp.dot(activ, down_local, preferred_element_type=jnp.float32)
    block_out = (
        lax.dynamic_slice_in_dim(resid, col_start, cols, 1)
        + lax.psum_scatter(
            down_part.astype(jnp.bfloat16), "mp", scatter_dimension=1, tiled=True
        ).astype(jnp.float32)
    ).astype(jnp.bfloat16)
    cotan = out_grad.astype(jnp.float32)
    grad_activ = against(out_grad, down_local)
    down_grad = inner(activ, out_grad)
    grad_gate = (grad_activ * lift * sigma * (1.0 + gate * (1.0 - sigma))).astype(jnp.bfloat16)
    grad_lift = (grad_activ * gate * sigma).astype(jnp.bfloat16)
    gate_up_grad = jnp.stack((inner(hidden_two, grad_gate), inner(hidden_two, grad_lift)))
    back_two = lax.psum(
        (against(grad_gate, gate_up_local[0]) + against(grad_lift, gate_up_local[1])).astype(
            jnp.bfloat16
        ),
        "mp",
    ).astype(jnp.float32)
    gain_two = jnp.sum(back_two * normed_two, axis=0)
    grad_resid = (
        cotan
        + scale_two * second_gain * back_two
        - resid * scale_two**3 * jnp.mean(resid * second_gain * back_two, axis=1, keepdims=True)
    )
    resid_low = grad_resid.astype(jnp.bfloat16)
    output_grad = inner(mixed, resid_low)
    grad_mixed = against(resid_low, output_local).reshape(seq_count, LEN, heads_here, VH)
    grad_query, grad_keys, grad_values = lax.map(
        mix_backward, (head_query, head_keys, head_values, numer, denom, grad_mixed)
    )
    grad_query = grad_query.reshape(tok_count, width)
    grad_keys = grad_keys.reshape(tok_count, width)
    grad_values = grad_values.reshape(tok_count, heads_here * VH)
    qk_grad = jnp.stack((inner(hidden_one, grad_query), inner(hidden_one, grad_keys)))
    value_grad = inner(hidden_one, grad_values)
    back_one = (
        against(grad_query, qk_local[0])
        + against(grad_keys, qk_local[1])
        + against(grad_values, value_local)
    )
    input_part = scale_one * first_gain * back_one - inputs * scale_one**3 * jnp.mean(
        inputs * first_gain * back_one, axis=1, keepdims=True
    )
    gains_grad = jnp.stack((jnp.sum(back_one * normed_one, axis=0), gain_two))
    input_grad = lax.dynamic_slice_in_dim(grad_resid, col_start, cols, 1) + lax.psum_scatter(
        input_part.astype(jnp.bfloat16), "mp", scatter_dimension=1, tiled=True
    ).astype(jnp.float32)
    qk_grad = lax.all_gather(qk_grad.astype(jnp.bfloat16), "mp", axis=2, tiled=True).astype(
        qk_grad.dtype
    )
    qk_share, value_share, output_share, gate_up_share, down_share, gains_share = (
        lax.psum_scatter(qk_grad, "dp", scatter_dimension=1, tiled=True),
        lax.psum_scatter(value_grad, "dp", scatter_dimension=0, tiled=True),
        lax.psum_scatter(output_grad, "dp", scatter_dimension=1, tiled=True),
        lax.psum_scatter(gate_up_grad, "dp", scatter_dimension=1, tiled=True),
        lax.psum_scatter(down_grad, "dp", scatter_dimension=1, tiled=True),
        lax.psum_scatter(gains_grad, "dp", scatter_dimension=1, tiled=True),
    )
    first_row = lax.psum(gains_share[0], "mp")
    gains_share = jnp.stack((first_row, gains_share[1]))
    spread_sum = (
        jnp.sum(value_share * value_share)
        + jnp.sum(output_share * output_share)
        + jnp.sum(gate_up_share * gate_up_share)
        + jnp.sum(down_share * down_share)
    )
    shared_sum = jnp.sum(qk_share * qk_share) + jnp.sum(gains_share * gains_share)
    total = lax.psum(spread_sum + shared_sum / groups, ("dp", "mp"))
    grad_norm = jnp.sqrt(total)
    clip = jnp.minimum(1.0, 1.0 / (grad_norm + 1e-06))
    qk_m, qk_v, qk_w, qk_a = adam_step(
        clip * qk_share, qk_first, qk_second, qk_weight, qk_average, 1.0 / math.sqrt(D)
    )
    value_m, value_v, value_w, value_a = adam_step(
        clip * value_share,
        value_first,
        value_second,
        value_weight,
        value_average,
        1.0 / math.sqrt(D),
    )
    output_m, output_v, output_w, output_a = adam_step(
        clip * output_share,
        output_first,
        output_second,
        output_weight,
        output_average,
        1.0 / math.sqrt(max(1, V_ALL * 16 // LEN)),
    )
    gate_up_m, gate_up_v, gate_up_w, gate_up_a = adam_step(
        clip * gate_up_share,
        gate_up_first,
        gate_up_second,
        gate_up_weight,
        gate_up_average,
        1.0 / math.sqrt(D),
    )
    down_m, down_v, down_w, down_a = adam_step(
        clip * down_share, down_first, down_second, down_weight, down_average, 1.0 / math.sqrt(FF)
    )
    gains_m, gains_v, gains_w, gains_a = adam_step(
        clip * gains_share, gains_first, gains_second, gains, gains_average, 0.4
    )
    return (
        block_out,
        input_grad,
        grad_norm,
        qk_m,
        qk_v,
        qk_w,
        qk_a,
        value_m,
        value_v,
        value_w,
        value_a,
        output_m,
        output_v,
        output_w,
        output_a,
        gate_up_m,
        gate_up_v,
        gate_up_w,
        gate_up_a,
        down_m,
        down_v,
        down_w,
        down_a,
        gains_m,
        gains_v,
        gains_w,
        gains_a,
    )


def solution(mesh):
    placed = (
        P("dp", None),
        P("dp", None),
        P(None, "dp", None),
        P(None, "dp", None),
        P(None, "dp", None),
        P(None, "dp", None),
        P("dp", "mp"),
        P("dp", "mp"),
        P("dp", "mp"),
        P("dp", "mp"),
        P("mp", "dp"),
        P("mp", "dp"),
        P("mp", "dp"),
        P("mp", "dp"),
        P(None, "dp", "mp"),
        P(None, "dp", "mp"),
        P(None, "dp", "mp"),
        P(None, "dp", "mp"),
        P("mp", "dp"),
        P("mp", "dp"),
        P("mp", "dp"),
        P("mp", "dp"),
        P(None, "dp"),
        P(None, "dp"),
        P(None, "dp"),
        P(None, "dp"),
    )
    return jax.shard_map(
        on_device,
        mesh=mesh,
        in_specs=placed,
        out_specs=(
            P("dp", "mp"),
            P("dp", "mp"),
            P(),
            P(None, "dp", None),
            P(None, "dp", None),
            P(None, "dp", None),
            P(None, "dp", None),
            P("dp", "mp"),
            P("dp", "mp"),
            P("dp", "mp"),
            P("dp", "mp"),
            P("mp", "dp"),
            P("mp", "dp"),
            P("mp", "dp"),
            P("mp", "dp"),
            P(None, "dp", "mp"),
            P(None, "dp", "mp"),
            P(None, "dp", "mp"),
            P(None, "dp", "mp"),
            P("mp", "dp"),
            P("mp", "dp"),
            P("mp", "dp"),
            P("mp", "dp"),
            P(None, "dp"),
            P(None, "dp"),
            P(None, "dp"),
            P(None, "dp"),
        ),
        check_vma=False,
    )
```

profile of v0, /device:TPU:0, one launch (start us, length us, event | category | flops | bytes accessed | tf_op | source)
XLA Modules:
  0.0 1489.0 jit_solution(11503148982517520819)
XLA Ops:
  9.9 22.2 %all_gather.21 = bf16[2,1024]{1,0:T(2,128)(2,1)S(1)} all-gather(bf16[2,128]{1,0:T(2,128)(2,1)S(1)} %convert_element_type.163), channel_id=1, replica_groups=mesh['dp'=8,'mp'=4] {'dp'}, dimensions={1}, use_global_device_ids=true | all-gather | bytes 4608 | tf_op jit(solution)/shard_map/all_gather | solution.py:121
  37.9 31.9 %all_gather.22 = bf16[1024,256]{1,0:T(8,128)(2,1)S(1)} all-gather(bf16[128,256]{1,0:T(8,128)(2,1)S(1)} %convert_element_type.165), channel_id=1, replica_groups=mesh['dp'=8,'mp'=4] {'dp'}, dimensions={0}, use_global_device_ids=true | all-gather | bytes 589824 | tf_op jit(solution)/shard_map/all_gather | solution.py:117
  86.5 28.1 %all_gather.24 = bf16[256,1024]{1,0:T(8,128)(2,1)} all-gather(bf16[256,128]{1,0:T(8,128)(2,1)S(1)} %convert_element_type.171), channel_id=1, replica_groups=mesh['dp'=8,'mp'=4] {'dp'}, dimensions={1}, use_global_device_ids=true | all-gather | bytes 589824 | tf_op jit(solution)/shard_map/all_gather | solution.py:118
  114.6 6.1 convolution_convert_fusion.3
  121.3 6.1 convolution_convert_fusion.4
  129.8 35.0 %while.30 = (s32[]{:T(128)}, f32[4,1024,4,64]{1,3,2,0:T(8,128)}, f32[4,1024,4]{1,2,0:T(4,128)S(1)}, bf16[4,1024,4,64]{1,3,2,0:T(8,128)(2,1)S(1)}, bf16[4,1024,4,...) while((s32[]{:T(128)}, f32[4,1024,4,64]{1,3,2,0:T(8,128)}, ...), condition=%wide.region_3.4_spmd, body=%wide.region_1.3_spmd.sunk | while | flops 706736128 | bytes 27052120 | solution.py:146
  181.0 148.5 %all-reduce.3.cloned.1.call-done = bf16[4096,1024]{1,0:T(8,128)(2,1)} async-done(((bf16[4096,1024]{1,0:T(8,128)(2,1)}), bf16[4096,1024]{1,0:T(8,128)(2,1)}) %all-reduce.3.cloned.1.call-update) | async-done | bytes 8388624 | tf_op jit(solution)/shard_map/psum | solution.py:149
  329.6 8.6 multiply_reduce_fusion
  338.1 10.8 multiply_convert_fusion.9
  348.9 42.7 %all-gather.7.cloned.1.call-done = bf16[2,1024,688]{1,2,0:T(8,128)(2,1)} async-done(((bf16[2,128,688]{1,2,0:T(8,128)(2,1)}), bf16[2,1024,688]{1,2,0:T(8,128)(2,1)}) %all-gather.7.cloned.1.call-update) | async-done | bytes 2818064 | tf_op jit(solution)/shard_map/all_gather | solution.py:119
  391.6 12.5 fusion.68
  404.1 8.8 fusion.67
  412.9 22.6 %all-gather.9.cloned.1.call-done = bf16[688,1024]{1,0:T(8,128)(2,1)} async-done(((bf16[688,128]{1,0:T(8,128)(2,1)}), bf16[688,1024]{1,0:T(8,128)(2,1)}) %all-gather.9.cloned.1.call-update) | async-done | bytes 1409040 | tf_op jit(solution)/shard_map/all_gather | solution.py:120
  435.5 22.1 %multiply_convert_fusion.10 = (bf16[4096,688]{0,1:T(8,128)(2,1)}, bf16[4096,688]{0,1:T(8,128)(2,1)}, bf16[4096,688]{0,1:T(8,128)(2,1)}) fusion(f32[4096,688]{0,1:T(8,128)} %fusion.67, f32[4096,688]{0,1:T(8,128)} %fusion.68, bf16[4096,1024]{1,0:T(8,128)(2,1)} %param.31, bf16[688,1024]{1,0:T(8,128)(2,1)} %all-gather.9.cloned.1.call-done), kind=kOutput, calls=%fused_computation.84 | convolution fusion | flops 5816451072 | bytes 49250304 | tf_op jit(solution)/shard_map/dot_general | solution.py:24
  457.6 13.2 fusion.66
  470.8 12.5 add_convert_fusion
  483.4 151.4 %all-reduce.5.cloned.1.call-done = bf16[4096,1024]{1,0:T(8,128)(2,1)} async-done(((bf16[4096,1024]{1,0:T(8,128)(2,1)}), bf16[4096,1024]{1,0:T(8,128)(2,1)}) %all-reduce.5.cloned.1.call-update) | async-done | bytes 8388624 | tf_op jit(solution)/shard_map/psum | solution.py:170
  634.8 12.0 fusion.55
  646.8 17.5 %fusion.53 = (f32[4096,1024]{1,0:T(8,128)S(1)}, f32[4096,1024]{1,0:T(8,128)}) fusion(bf16[4096,1024]{1,0:T(8,128)(2,1)} %all-reduce.5.cloned.1.call-done, bf16[4096,1024]{1,0:T(8,128)(2,1)} %param.31, f32[4096]{0:T(1024)S(1)} %broadcast_multiply_fusion.1, f32[4096]{0:T(1024)S(1)} %get-tuple-element.439, f32[1024]{0:T(1024)S(1)} %bitcast.225, ...), kind=kLoop, calls=%fused_computation.71 | loop fusion | flops 46137344 | bytes 67162112 | tf_op jit(solution)/shard_map/sub | solution.py:178
  664.3 5.7 copy-done.5
  674.4 6.0 reshape.148
  680.5 141.2 %while.31 = (s32[]{:T(128)}, bf16[4,1024,4,16]{1,3,2,0:T(8,128)(2,1)}, bf16[4,1024,4,16]{1,3,2,0:T(8,128)(2,1)}, bf16[4,1024,4,64]{1,3,2,0:T(8,128)(2,1)}, bf16[...) while((s32[]{:T(128)}, ...), condition=%wide.region_11.12_spmd, body=%wide.region_9.11_spmd.sunk | while | flops 1535123456 | bytes 167644336 | solution.py:185
  690.7 5.7 copy-done
  701.1 8.3 multiply_convert_fusion.16
  725.8 5.7 copy-done
  736.3 8.3 multiply_convert_fusion.16
  761.0 5.7 copy-done
  771.4 8.3 multiply_convert_fusion.16
  806.6 8.3 multiply_convert_fusion.16
  832.6 9.6 fusion.75
  842.3 9.3 fusion.74
  851.6 18.5 %fusion.51 = (f32[1024]{0:T(1024)S(1)}, f32[4096]{0:T(1024)S(1)}, f32[4096,1024]{1,0:T(8,128)}) fusion(bf16[4096,1024]{1,0:T(8,128)(2,1)S(1)} %bitcast.205, f32[4096]{0:T(1024)S(1)} %copy-done.29, f32[1024]{0:T(1024)S(1)} %bitcast.221, bf16[4096,256]{0,1:T(8,128)(2,1)S(1)} %bitcast.208, bf16[1024,256]{1,0:T(8,128)(2,1)} %copy-done.19, ...), kind=kOutput, calls=%fused_computation.69 | convolution fusion | flops 2185227264 | bytes 61382656 | tf_op jit(solution)/shard_map/dot_general | solution.py:24
  871.2 11.6 fusion.92
  882.9 9.2 fusion.62
  892.1 7.4 fusion.91
  902.5 10.3 convolution_bitcast_fusion
  912.8 10.1 convolution_bitcast_fusion.1
  926.0 11.8 convolution_convert_fusion
  938.5 12.5 fusion.59
  953.7 6.1 psum.30
  960.4 50.7 %reduce-scatter.21.cloned.1.call-done = f32[688,128]{1,0:T(8,128)} async-done(((f32[688,1024]{1,0:T(8,128)}), f32[688,128]{1,0:T(8,128)}) %reduce-scatter.21.cloned.1.call-update) | async-done | bytes 352272 | tf_op jit(solution)/shard_map/reduce_scatter | solution.py:213
  1012.9 64.5 %reduce-scatter.17.cloned.1.call-done = f32[256,128]{1,0:T(8,128)} async-done(((f32[256,1024]{1,0:T(8,128)}), f32[256,128]{1,0:T(8,128)}) %reduce-scatter.17.cloned.1.call-update) | async-done | bytes 131088 | tf_op jit(solution)/shard_map/reduce_scatter | solution.py:211
  1078.9 64.1 %reduce-scatter.15.cloned.1.call-done = f32[128,256]{1,0:T(8,128)} async-done(((f32[1024,256]{1,0:T(8,128)}), f32[128,256]{1,0:T(8,128)}) %reduce-scatter.15.cloned.1.call-update) | async-done | bytes 131088 | tf_op jit(solution)/shard_map/reduce_scatter | solution.py:210
  1145.9 69.1 %reduce-scatter.23.cloned.1.call-done = f32[2,128,256]{1,2,0:T(8,128)} async-done(((f32[2,1024,256]{1,2,0:T(8,128)}), f32[2,128,256]{1,2,0:T(8,128)}) %reduce-scatter.23.cloned.1.call-update) | async-done | bytes 262160 | tf_op jit(solution)/shard_map/reduce_scatter | solution.py:209
  1217.9 108.5 %reduce-scatter.19.cloned.1.call-done = f32[2,128,688]{1,2,0:T(8,128)} async-done(((f32[2,1024,688]{1,2,0:T(8,128)}), f32[2,128,688]{1,2,0:T(8,128)}) %reduce-scatter.19.cloned.1.call-update) | async-done | bytes 704528 | tf_op jit(solution)/shard_map/reduce_scatter | solution.py:212
  1329.7 40.8 %psum.31 = f32[]{:T(128)} all-reduce(f32[]{:T(128)S(6)} %add.280), channel_id=1, replica_groups=mesh['dp'=8,'mp'=4] {'dp','mp'}, use_global_device_ids=true, to_apply=%region_29.30 | all-reduce | flops 1 | bytes 8 | tf_op jit(solution)/shard_map/psum | solution.py:225
  1390.8 10.6 reduce-scatter.11.cloned.1.call-done
  1406.0 69.6 %reduce-scatter.13.cloned.1.call-done = bf16[4096,256]{1,0:T(8,128)(2,1)} async-done(((bf16[4096,1024]{1,0:T(8,128)(2,1)}), bf16[4096,256]{1,0:T(8,128)(2,1)}) %reduce-scatter.13.cloned.1.call-update) | async-done | bytes 2097168 | tf_op jit(solution)/shard_map/reduce_scatter | solution.py:202
  (246 shorter events, 233.1 us)
Async XLA Ops:
  7.2 30.7 %copy-start.24 = (f32[128,256]{1,0:T(8,128)S(1)}, f32[128,256]{1,0:T(8,128)}, u32[]{:S(2)}) copy-start(f32[128,256]{1,0:T(8,128)} %param.36) | copy-start | bytes 393220
  7.2 30.7 %copy-start.26 = (f32[256,128]{1,0:T(8,128)S(1)}, f32[256,128]{1,0:T(8,128)}, u32[]{:S(2)}) copy-start(f32[256,128]{1,0:T(8,128)} %param.40) | copy-start | bytes 393220
  7.2 107.4 %all-gather.5.cloned.1.call-start = ((), (), s32[]{:S(2)}) async-start(), calls=%async_computation.8 | async-start | bytes 1179648 | tf_op jit(solution)/shard_map/all_gather | solution.py:116
  9.0 320.6 %all-reduce.3.cloned.1.call-start = ((), (), s32[]{:S(2)}) async-start(), calls=%async_computation.9 | async-start | bytes 16777216 | tf_op jit(solution)/shard_map/psum | solution.py:149
  9.0 60.8 %copy-start.1 = (bf16[4096,1024]{1,0:T(8,128)(2,1)S(1)}, bf16[4096,1024]{1,0:T(8,128)(2,1)}, u32[]{:S(2)}) copy-start(bf16[4096,1024]{1,0:T(8,128)(2,1)} %param.30) | copy-start | bytes 25165828
  32.2 40.0 %copy-start.34 = (f32[1,1024]{1,0:T(1,128)}, f32[1,1024]{1,0:T(1,128)S(1)}, u32[]{:S(2)}) copy-start(f32[1,1024]{1,0:T(1,128)S(1)} %get-tuple-element.441) | copy-start | bytes 12292
  37.9 32.0 %copy-start.28 = (f32[4096]{0:T(1024)}, f32[4096]{0:T(1024)S(1)}, u32[]{:S(2)}) copy-start(f32[4096]{0:T(1024)S(1)} %get-tuple-element.438) | copy-start | bytes 49156
  164.8 6.5 copy-start.30
  164.8 13.5 copy-start.6
  164.8 13.5 copy-start.12
  164.8 13.5 copy-start.13
  164.8 7.8 copy-start.14
  178.3 213.3 %all-gather.7.cloned.1.call-start = ((), (), s32[]{:S(2)}) async-start(), calls=%async_computation.10 | async-start | bytes 3170304 | tf_op jit(solution)/shard_map/all_gather | solution.py:119
  180.2 255.3 %all-gather.9.cloned.1.call-start = ((), (), s32[]{:S(2)}) async-start(), calls=%async_computation.11 | async-start | bytes 1585152 | tf_op jit(solution)/shard_map/all_gather | solution.py:120
  181.0 453.8 %all-reduce.5.cloned.1.call-start = ((), (), s32[]{:S(2)}) async-start(), calls=%async_computation.13 | async-start | bytes 16777216 | tf_op jit(solution)/shard_map/psum | solution.py:170
  391.6 12.5 copy-start.10
  391.6 12.5 copy-start.40
  457.6 13.2 copy-start.42
  483.3 416.3 %all-gather.11.cloned.1.call-start = ((), (), s32[]{:S(2)}) async-start(), calls=%async_computation.19 | async-start | bytes 1310720 | tf_op jit(solution)/shard_map/all_gather | solution.py:205
  646.8 23.2 %copy-start.15 = (bf16[256,1024]{1,0:T(8,128)(2,1)S(1)}, bf16[256,1024]{1,0:T(8,128)(2,1)}, u32[]{:S(2)}) copy-start(bf16[256,1024]{1,0:T(8,128)(2,1)} %all_gather.24) | copy-start | bytes 1572868
  664.3 5.7 copy-start.5
  684.1 6.5 copy-start.4
  719.3 6.5 copy-start.4
  754.5 6.5 copy-start.4
  789.6 6.5 copy-start.4
  821.7 6.3 copy-start.3
  825.9 25.6 %copy-start.9 = (bf16[32,8,4,1024]{3,1,2,0:T(8,128)(2,1)}, bf16[32,8,4,1024]{3,1,2,0:T(8,128)(2,1)S(1)}, u32[]{:S(2)}) copy-start(bf16[32,8,4,1024]{3,1,2,0:T(8,128)(2,1)S(1)} %copy.128) | copy-start | bytes 6291460
  832.6 120.0 %reduce-scatter.25.cloned.1.call-start = ((), (), s32[]{:S(2)}) async-start(), calls=%async_computation.21 | async-start | bytes 589824
  832.6 18.9 %slice-start = ((s8[8388608]{0:T(1024)(128)(4,1)}), s8[4194304]{0:T(1024)(128)(4,1)S(1)}, s32[]{:S(2)}) async-start(s8[8388608]{0:T(1024)(128)(4,1)} %bitcast.204), calls=%async_computation.22 | async-start | bytes 8388608
  842.3 9.3 slice-start.1
  842.3 9.3 copy-start.29
  842.3 9.3 copy-start.35
  851.6 18.5 %copy-start.37 = (f32[1024]{0:T(1024)S(1)}, f32[1024]{0:T(1024)}, u32[]{:S(2)}) copy-start(f32[1024]{0:T(1024)} %get-tuple-element.368) | copy-start | bytes 12292
  871.1 140.0 %reduce-scatter.21.cloned.1.call-start = ((), (), s32[]{:S(2)}) async-start(), calls=%async_computation.18 | async-start | bytes 3170304 | tf_op jit(solution)/shard_map/reduce_scatter | solution.py:213
  871.2 11.7 copy-start.8
  882.9 194.5 %reduce-scatter.17.cloned.1.call-start = ((), (), s32[]{:S(2)}) async-start(), calls=%async_computation.16 | async-start | bytes 1179648 | tf_op jit(solution)/shard_map/reduce_scatter | solution.py:211
  892.1 250.9 %reduce-scatter.15.cloned.1.call-start = ((), (), s32[]{:S(2)}) async-start(), calls=%async_computation.15 | async-start | bytes 1179648 | tf_op jit(solution)/shard_map/reduce_scatter | solution.py:210
  899.6 315.4 %reduce-scatter.23.cloned.1.call-start = ((), (), s32[]{:S(2)}) async-start(), calls=%async_computation.20 | async-start | bytes 2359296 | tf_op jit(solution)/shard_map/reduce_scatter | solution.py:209
  902.5 423.9 %reduce-scatter.19.cloned.1.call-start = ((), (), s32[]{:S(2)}) async-start(), calls=%async_computation.17 | async-start | bytes 6340608 | tf_op jit(solution)/shard_map/reduce_scatter | solution.py:212
  926.0 475.4 %reduce-scatter.11.cloned.1.call-start = ((), (), s32[]{:S(2)}) async-start(), calls=%async_computation.12 | async-start | bytes 10485760 | tf_op jit(solution)/shard_map/reduce_scatter | solution.py:160
  937.8 537.8 %reduce-scatter.13.cloned.1.call-start = ((), (), s32[]{:S(2)}) async-start(), calls=%async_computation.14 | async-start | bytes 10485760 | tf_op jit(solution)/shard_map/reduce_scatter | solution.py:202
  951.0 429.8 %copy-start.25 = (f32[128,256]{1,0:T(8,128)S(1)}, f32[128,256]{1,0:T(8,128)}, u32[]{:S(2)}) copy-start(f32[128,256]{1,0:T(8,128)} %param.36) | copy-start | bytes 393220
  951.1 433.7 %copy-start.21 = (f32[688,128]{1,0:T(8,128)S(1)}, f32[688,128]{1,0:T(8,128)}, u32[]{:S(2)}) copy-start(f32[688,128]{1,0:T(8,128)} %param.48) | copy-start | bytes 1056772
  951.1 436.2 %copy-start.17 = (f32[2,128,688]{1,2,0:T(8,128)S(1)}, f32[2,128,688]{1,2,0:T(8,128)}, u32[]{:S(2)}) copy-start(f32[2,128,688]{1,2,0:T(8,128)} %param.44) | copy-start | bytes 2113540
  953.7 417.5 %copy-start.38 = (f32[1,128]{1,0:T(1,128)}, f32[1,128]{1,0:T(1,128)S(1)}, u32[]{:S(2)}) copy-start(f32[1,128]{1,0:T(1,128)S(1)} %copy.124) | copy-start | bytes 1540
  959.8 411.4 %copy-start.39 = (f32[1,128]{1,0:T(1,128)}, f32[1,128]{1,0:T(1,128)S(1)}, u32[]{:S(2)}) copy-start(f32[1,128]{1,0:T(1,128)S(1)} %psum.30) | copy-start | bytes 1540
  1011.1 373.6 %copy-start.22 = (f32[688,128]{1,0:T(8,128)S(1)}, f32[688,128]{1,0:T(8,128)}, u32[]{:S(2)}) copy-start(f32[688,128]{1,0:T(8,128)} %reduce-scatter.21.cloned.1.call-done) | copy-start | bytes 1056772
  1326.4 60.9 %copy-start.18 = (f32[2,128,688]{1,2,0:T(8,128)S(1)}, f32[2,128,688]{1,2,0:T(8,128)}, u32[]{:S(2)}) copy-start(f32[2,128,688]{1,2,0:T(8,128)} %reduce-scatter.19.cloned.1.call-done) | copy-start | bytes 2113540
  (17 other events, 44.5 us)
Sparse Core Ops, SparseCore 0:
  10.8 46.0 all-gather.4
  178.4 151.0 all-reduce.2
  332.2 59.3 all-gather.6
  394.1 41.3 all-gather.8
  483.5 151.3 all-reduce.4
  832.7 16.8 all-gather.10
  871.3 62.0 reduce-scatter.24
  937.9 73.2 reduce-scatter.20
  1014.9 62.3 reduce-scatter.16
  1080.6 62.3 reduce-scatter.14
  1147.6 67.3 reduce-scatter.22
  1218.9 107.4 reduce-scatter.18
  1329.2 72.2 reduce-scatter.10
  1403.8 71.7 reduce-scatter.12
where the time goes:
time: 1500 us; the launch traced here: 1490 us
  waiting for transfers between devices  802 us (53%)
  matrix products  319 us (21%)
  other arithmetic  131 us (9%)
  blocking collectives  129 us (9%)
  local copies, waits for them, and re-layouts  84.8 us (6%)
  between operations  20.9 us (1%)
    psum x1, waiting for transfers between devices, on_device(): lax.psum((against(grad_gate, gate_up_local[0]) + against(grad_lift, gate_...  151 us
    psum x1, waiting for transfers between devices, on_device(): lax.psum(attn_part.astype(jnp.bfloat16), 'mp').astype(jnp.float32)  149 us
    reduce_scatter x1, waiting for transfers between devices, on_device(): lax.psum_scatter(gate_up_grad, 'dp', scatter_dimension=1, tiled=True)  108 us
    dot_general x7, matrix products, against(): lax.dot_general(left, right, (((1,), (1,)), ((), ())), preferred_element_...  89.6 us
    reduce_scatter x1, waiting for transfers between devices, on_device(): lax.psum_scatter(input_part.astype(jnp.bfloat16), 'mp', scatter_dimension...  69.6 us
    reduce_scatter x1, waiting for transfers between devices, on_device(): lax.psum_scatter(qk_grad, 'dp', scatter_dimension=1, tiled=True)  69.1 us
    reduce_scatter x1, waiting for transfers between devices, on_device(): lax.psum_scatter(output_grad, 'dp', scatter_dimension=1, tiled=True)  64.5 us
    reduce_scatter x1, waiting for transfers between devices, on_device(): lax.psum_scatter(value_grad, 'dp', scatter_dimension=0, tiled=True)  64.1 us
  transfers between devices with their start and end apart: 14, of which 11 were waited for; matrix products, arithmetic and copies ran while one was open for 14% of the time, Pallas kernels for 0%

commit v1 on v0

--- a/solution.py
+++ b/solution.py
@@ -12,6 +12,19 @@
 V_ALL = 1024
 LEN = 1024
 STEP = 5
+
+
+def collect(value, axis, dim):
+    ways = lax.axis_size(axis)
+    up = [(d, (d + 1) % ways) for d in range(ways)]
+    down = [(d, (d - 1) % ways) for d in range(ways)]
+    earlier, later = ([value], [value])
+    for _ in range(ways // 2):
+        earlier.append(lax.ppermute(earlier[-1], axis, up))
+    for _ in range((ways - 1) // 2):
+        later.append(lax.ppermute(later[-1], axis, down))
+    line = jnp.concatenate([*earlier[::-1], *later[1:]], axis=dim)
+    return jnp.roll(line, (lax.axis_index(axis) - ways // 2) * value.shape[dim], axis=dim)
 
 
 def inner(left, right):
@@ -116,7 +129,7 @@
         lax.all_gather(qk_weight.astype(jnp.bfloat16), "dp", axis=1, tiled=True),
         lax.all_gather(value_weight.astype(jnp.bfloat16), "dp", axis=0, tiled=True),
         lax.all_gather(output_weight.astype(jnp.bfloat16), "dp", axis=1, tiled=True),
-        lax.all_gather(gate_up_weight.astype(jnp.bfloat16), "dp", axis=1, tiled=True),
+        collect(gate_up_weight.astype(jnp.bfloat16), "dp", 1),
         lax.all_gather(down_weight.astype(jnp.bfloat16), "dp", axis=1, tiled=True),
         lax.all_gather(gains.astype(jnp.bfloat16), "dp", axis=1, tiled=True),
     )

time: 1500 us -> 1450 us (0.967)
  waiting for transfers between devices: 802 us -> 708 us
  local copies, waits for them, and re-layouts: 84.8 us -> 104 us
    all_gather x1 -> x0, waiting for transfers between devices: 42.7 us -> none  [on_device(): lax.all_gather(gate_up_weight.astype(jnp.bfloat16), 'dp', axis=1, tiled=T...]
    psum x1, waiting for transfers between devices: 149 us -> 119 us  [on_device(): lax.psum(attn_part.astype(jnp.bfloat16), 'mp').astype(jnp.float32)]
    all_gather x1, waiting for transfers between devices: 22.6 us -> 0.01 us  [on_device(): lax.all_gather(down_weight.astype(jnp.bfloat16), 'dp', axis=1, tiled=True)]
    unnamed x101 -> x116, local copies, waits for them, and re-layouts: 22.9 us -> 38.4 us
  transfers between devices with their start and end apart: 14 -> 20, of which waited for: 11 -> 9; matrix products, arithmetic and copies ran while one was open for 14% -> 19% of each run, Pallas kernels for 0% -> 0%
where the time goes in v1:
time: 1450 us; the launch traced here: 1440 us
  waiting for transfers between devices  708 us (49%)
  matrix products  319 us (22%)
  blocking collectives  143 us (10%)
  other arithmetic  131 us (9%)
  local copies, waits for them, and re-layouts  104 us (7%)
  between operations  21 us (1%)
    psum x1, waiting for transfers between devices, on_device(): lax.psum((against(grad_gate, gate_up_local[0]) + against(grad_lift, gate_...  153 us
    psum x1, waiting for transfers between devices, on_device(): lax.psum(attn_part.astype(jnp.bfloat16), 'mp').astype(jnp.float32)  119 us
    reduce_scatter x1, waiting for transfers between devices, on_device(): lax.psum_scatter(gate_up_grad, 'dp', scatter_dimension=1, tiled=True)  109 us
    dot_general x7, matrix products, against(): lax.dot_general(left, right, (((1,), (1,)), ((), ())), preferred_element_...  79 us
    reduce_scatter x1, waiting for transfers between devices, on_device(): lax.psum_scatter(input_part.astype(jnp.bfloat16), 'mp', scatter_dimension...  69.7 us
    reduce_scatter x1, waiting for transfers between devices, on_device(): lax.psum_scatter(qk_grad, 'dp', scatter_dimension=1, tiled=True)  68.7 us
    reduce_scatter x1, waiting for transfers between devices, on_device(): lax.psum_scatter(output_grad, 'dp', scatter_dimension=1, tiled=True)  64.7 us
    reduce_scatter x1, waiting for transfers between devices, on_device(): lax.psum_scatter(value_grad, 'dp', scatter_dimension=0, tiled=True)  64.3 us
  transfers between devices with their start and end apart: 20, of which 9 were waited for; matrix products, arithmetic and copies ran while one was open for 19% of the time, Pallas kernels for 0%

profile of v1, /device:TPU:0, one launch (start us, length us, event | category | flops | bytes accessed | tf_op | source)
XLA Modules:
  0.0 1439.5 jit_solution(2565225556244591234)
XLA Ops:
  10.1 6.0 collective-permute-start.4
  18.7 25.9 %all_gather.18 = bf16[2,1024]{1,0:T(2,128)(2,1)S(1)} all-gather(bf16[2,128]{1,0:T(2,128)(2,1)S(1)} %convert_element_type.163), channel_id=1, replica_groups=mesh['dp'=8,'mp'=4] {'dp'}, dimensions={1}, use_global_device_ids=true | all-gather | bytes 4608 | tf_op jit(solution)/shard_map/all_gather | solution.py:134
  52.8 37.8 %all_gather.19 = bf16[1024,256]{1,0:T(8,128)(2,1)S(1)} all-gather(bf16[128,256]{1,0:T(8,128)(2,1)S(1)} %convert_element_type.165), channel_id=1, replica_groups=mesh['dp'=8,'mp'=4] {'dp'}, dimensions={0}, use_global_device_ids=true | all-gather | bytes 589824 | tf_op jit(solution)/shard_map/all_gather | solution.py:130
  101.9 32.4 %all_gather.21 = bf16[256,1024]{1,0:T(8,128)(2,1)} all-gather(bf16[256,128]{1,0:T(8,128)(2,1)S(1)} %convert_element_type.171), channel_id=1, replica_groups=mesh['dp'=8,'mp'=4] {'dp'}, dimensions={1}, use_global_device_ids=true | all-gather | bytes 589824 | tf_op jit(solution)/shard_map/all_gather | solution.py:131
  136.3 6.1 convolution_convert_fusion.3
  143.0 6.1 convolution_convert_fusion.4
  151.5 37.4 %while.30 = (s32[]{:T(128)}, f32[4,1024,4,64]{1,3,2,0:T(8,128)}, f32[4,1024,4]{1,2,0:T(4,128)}, bf16[4,1024,4,64]{1,3,2,0:T(8,128)(2,1)S(1)}, bf16[4,1024,4,16]{...) while((s32[]{:T(128)}, f32[4,1024,4,64]{1,3,2,0:T(8,128)}, ...), condition=%wide.region_3.4_spmd, body=%wide.region_1.3_spmd.sunk | while | flops 706736128 | bytes 27052120 | solution.py:159
  225.9 11.8 fusion.95
  237.7 118.8 %all-reduce.3.cloned.1.call-done = bf16[4096,1024]{1,0:T(8,128)(2,1)} async-done(((bf16[4096,1024]{1,0:T(8,128)(2,1)}), bf16[4096,1024]{1,0:T(8,128)(2,1)}) %all-reduce.3.cloned.1.call-update) | async-done | bytes 8388624 | tf_op jit(solution)/shard_map/psum | solution.py:162
  356.6 8.6 multiply_reduce_fusion
  365.1 7.5 multiply_convert_fusion.9
  375.9 10.0 fusion.68
  386.0 21.7 %multiply_convert_fusion.11 = (bf16[4096,688]{0,1:T(8,128)(2,1)}, bf16[4096,688]{0,1:T(8,128)(2,1)}, bf16[4096,688]{0,1:T(8,128)(2,1)}) fusion(f32[4096,688]{0,1:T(8,128)} %fusion.95, f32[4096,688]{0,1:T(8,128)} %fusion.68, bf16[4096,1024]{1,0:T(8,128)(2,1)} %copy-done.12, bf16[2,2048,688]{1,2,0:T(8,128)(2,1)} %constant_dynamic-update-slice_fusion, ...), kind=kOutput, calls=%fused_computation.85 | convolution fusion | flops 5816451072 | bytes 49250308 | tf_op jit(solution)/shard_map/dot_general | solution.py:166
  407.6 12.6 fusion.67
  420.2 12.8 add_convert_fusion
  433.1 153.1 %all-reduce.5.cloned.1.call-done = bf16[4096,1024]{1,0:T(8,128)(2,1)} async-done(((bf16[4096,1024]{1,0:T(8,128)(2,1)}), bf16[4096,1024]{1,0:T(8,128)(2,1)}) %all-reduce.5.cloned.1.call-update) | async-done | bytes 8388624 | tf_op jit(solution)/shard_map/psum | solution.py:183
  586.2 12.4 fusion.55
  598.6 17.5 %fusion.53 = (f32[4096,1024]{1,0:T(8,128)S(1)}, f32[4096,1024]{1,0:T(8,128)}) fusion(bf16[4096,1024]{1,0:T(8,128)(2,1)} %all-reduce.5.cloned.1.call-done, bf16[4096,1024]{1,0:T(8,128)(2,1)} %param.31, f32[4096]{0:T(1024)S(1)} %broadcast_multiply_fusion.1, f32[4096]{0:T(1024)S(1)} %get-tuple-element.439, f32[1024]{0:T(1024)S(1)} %bitcast.227, ...), kind=kLoop, calls=%fused_computation.71 | loop fusion | flops 46137344 | bytes 67162112 | tf_op jit(solution)/shard_map/sub | solution.py:191
  616.1 5.7 copy-done.5
  626.2 6.0 reshape.148
  632.2 140.9 %while.31 = (s32[]{:T(128)}, bf16[4,1024,4,16]{1,3,2,0:T(8,128)(2,1)}, bf16[4,1024,4,16]{1,3,2,0:T(8,128)(2,1)}, bf16[4,1024,4,64]{1,3,2,0:T(8,128)(2,1)}, bf16[...) while((s32[]{:T(128)}, ...), condition=%wide.region_11.12_spmd, body=%wide.region_9.11_spmd.sunk | while | flops 1535123456 | bytes 167644336 | solution.py:198
  642.0 5.7 copy-done
  652.5 8.3 multiply_convert_fusion.16
  677.2 5.7 copy-done
  687.7 8.3 multiply_convert_fusion.16
  712.4 5.7 copy-done
  722.8 8.3 multiply_convert_fusion.16
  747.6 5.7 copy-done
  758.0 8.3 multiply_convert_fusion.16
  784.0 9.6 fusion.75
  793.7 9.3 fusion.74
  803.0 18.5 %fusion.51 = (f32[1024]{0:T(1024)S(1)}, f32[4096]{0:T(1024)S(1)}, f32[4096,1024]{1,0:T(8,128)}) fusion(bf16[4096,1024]{1,0:T(8,128)(2,1)S(1)} %bitcast.207, f32[4096]{0:T(1024)S(1)} %copy-done.32, f32[1024]{0:T(1024)S(1)} %bitcast.223, bf16[4096,256]{0,1:T(8,128)(2,1)S(1)} %bitcast.210, bf16[1024,256]{1,0:T(8,128)(2,1)} %copy-done.19, ...), kind=kOutput, calls=%fused_computation.69 | convolution fusion | flops 2185227264 | bytes 61382656 | tf_op jit(solution)/shard_map/dot_general | solution.py:37
  822.6 11.6 fusion.97
  834.4 9.1 fusion.62
  843.6 7.4 fusion.96
  853.9 10.3 convolution_bitcast_fusion.1
  864.3 10.1 convolution_bitcast_fusion
  877.4 11.8 convolution_convert_fusion
  890.0 12.5 fusion.59
  905.1 6.1 psum.30
  911.9 49.7 %reduce-scatter.21.cloned.1.call-done = f32[688,128]{1,0:T(8,128)} async-done(((f32[688,1024]{1,0:T(8,128)}), f32[688,128]{1,0:T(8,128)}) %reduce-scatter.21.cloned.1.call-update) | async-done | bytes 352272 | tf_op jit(solution)/shard_map/reduce_scatter | solution.py:226
  963.3 64.7 %reduce-scatter.17.cloned.1.call-done = f32[256,128]{1,0:T(8,128)} async-done(((f32[256,1024]{1,0:T(8,128)}), f32[256,128]{1,0:T(8,128)}) %reduce-scatter.17.cloned.1.call-update) | async-done | bytes 131088 | tf_op jit(solution)/shard_map/reduce_scatter | solution.py:224
  1029.5 64.3 %reduce-scatter.15.cloned.1.call-done = f32[128,256]{1,0:T(8,128)} async-done(((f32[1024,256]{1,0:T(8,128)}), f32[128,256]{1,0:T(8,128)}) %reduce-scatter.15.cloned.1.call-update) | async-done | bytes 131088 | tf_op jit(solution)/shard_map/reduce_scatter | solution.py:223
  1096.7 68.7 %reduce-scatter.23.cloned.1.call-done = f32[2,128,256]{1,2,0:T(8,128)} async-done(((f32[2,1024,256]{1,2,0:T(8,128)}), f32[2,128,256]{1,2,0:T(8,128)}) %reduce-scatter.23.cloned.1.call-update) | async-done | bytes 262160 | tf_op jit(solution)/shard_map/reduce_scatter | solution.py:222
  1168.3 108.7 %reduce-scatter.19.cloned.1.call-done = f32[2,128,688]{1,2,0:T(8,128)} async-done(((f32[2,1024,688]{1,2,0:T(8,128)}), f32[2,128,688]{1,2,0:T(8,128)}) %reduce-scatter.19.cloned.1.call-update) | async-done | bytes 704528 | tf_op jit(solution)/shard_map/reduce_scatter | solution.py:225
  1280.2 40.8 %psum.31 = f32[]{:T(128)} all-reduce(f32[]{:T(128)S(6)} %add.293), channel_id=1, replica_groups=mesh['dp'=8,'mp'=4] {'dp','mp'}, use_global_device_ids=true, to_apply=%region_29.30 | all-reduce | flops 1 | bytes 8 | tf_op jit(solution)/shard_map/psum | solution.py:238
  1341.3 10.5 reduce-scatter.11.cloned.1.call-done
  1356.4 69.7 %reduce-scatter.13.cloned.1.call-done = bf16[4096,256]{1,0:T(8,128)(2,1)} async-done(((bf16[4096,1024]{1,0:T(8,128)(2,1)}), bf16[4096,256]{1,0:T(8,128)(2,1)}) %reduce-scatter.13.cloned.1.call-update) | async-done | bytes 2097168 | tf_op jit(solution)/shard_map/reduce_scatter | solution.py:215
  (275 shorter events, 255.7 us)
Async XLA Ops:
  7.2 129.1 %all-gather.4.cloned.1.call-start = ((), (), s32[]{:S(2)}) async-start(), calls=%async_computation.8 | async-start | bytes 1179648 | tf_op jit(solution)/shard_map/all_gather | solution.py:129
  8.9 217.0 %all-gather.6.cloned.1.call-start = ((), (), s32[]{:S(2)}) async-start(), calls=%async_computation.10 | async-start | bytes 1585152 | tf_op jit(solution)/shard_map/all_gather | solution.py:133
  10.1 124.2 %collective-permute-start.4 = (bf16[2,128,688]{1,2,0:T(8,128)(2,1)S(1)}, bf16[2,128,688]{1,2,0:T(8,128)(2,1)S(1)}, u32[]{:S(2)}, u32[]{:S(2)}) collective-permute-start(bf16[2,128,688]{1,2,0:T(8,128)(2,1)S(1)} %convert_element_type.175), channel_id=1, source_target_pairs={{0,28},{4,0},{8,4},{12,8},{16,12},{20,16},{24,20},{28,24},{1,29},{... | collective-permute-start | bytes 1056776 | tf_op jit(solution)/shard_map/ppermute | solution.py:25
  16.1 34.3 %collective-permute-start = (bf16[2,128,688]{1,2,0:T(8,128)(2,1)S(1)}, bf16[2,128,688]{1,2,0:T(8,128)(2,1)S(1)}, u32[]{:S(2)}, u32[]{:S(2)}) collective-permute-start(bf16[2,128,688]{1,2,0:T(8,128)(2,1)S(1)} %convert_element_type.175), channel_id=1, source_target_pairs={{0,4},{4,8},{8,12},{12,16},{16,20},{20,24},{24,28},{28,0},{1,5},{5... | collective-permute-start | bytes 1056776 | tf_op jit(solution)/shard_map/ppermute | solution.py:23
  17.8 338.7 %all-reduce.3.cloned.1.call-start = ((), (), s32[]{:S(2)}) async-start(), calls=%async_computation.9 | async-start | bytes 16777216 | tf_op jit(solution)/shard_map/psum | solution.py:162
  17.9 32.6 %copy-start.1 = (bf16[4096,1024]{1,0:T(8,128)(2,1)S(1)}, bf16[4096,1024]{1,0:T(8,128)(2,1)}, u32[]{:S(2)}) copy-start(bf16[4096,1024]{1,0:T(8,128)(2,1)} %param.30) | copy-start | bytes 25165828
  50.4 40.1 %collective-permute-start.1 = (bf16[2,128,688]{1,2,0:T(8,128)(2,1)S(1)}, bf16[2,128,688]{1,2,0:T(8,128)(2,1)S(1)}, u32[]{:S(2)}, u32[]{:S(2)}) collective-permute-start(bf16[2,128,688]{1,2,0:T(8,128)(2,1)S(1)} %collective-permute-done), channel_id=1, source_target_pairs={{0,4},{4,8},{8,12},{12,16},{16,20},{20,24},{24,28},{28,0},{1,5},{5... | collective-permute-start | bytes 1056776 | tf_op jit(solution)/shard_map/ppermute | solution.py:23
  52.8 40.2 %copy-start.2 = (bf16[4096,1024]{1,0:T(8,128)(2,1)}, bf16[4096,1024]{1,0:T(8,128)(2,1)S(1)}, u32[]{:S(2)}) copy-start(bf16[4096,1024]{1,0:T(8,128)(2,1)S(1)} %fusion.50) | copy-start | bytes 25165828
  90.6 45.5 %collective-permute-start.2 = (bf16[2,128,688]{1,2,0:T(8,128)(2,1)S(1)}, bf16[2,128,688]{1,2,0:T(8,128)(2,1)}, u32[]{:S(2)}, u32[]{:S(2)}) collective-permute-start(bf16[2,128,688]{1,2,0:T(8,128)(2,1)S(1)} %collective-permute-done.1), channel_id=1, source_target_pairs={{0,4},{4,8},{8,12},{12,16},{16,20},{20,24},{24,28},{28,0},{1,5},{5... | collective-permute-start | bytes 1056776 | tf_op jit(solution)/shard_map/ppermute | solution.py:23
  134.3 68.1 %collective-permute-start.5 = (bf16[2,128,688]{1,2,0:T(8,128)(2,1)S(1)}, bf16[2,128,688]{1,2,0:T(8,128)(2,1)}, u32[]{:S(2)}, u32[]{:S(2)}) collective-permute-start(bf16[2,128,688]{1,2,0:T(8,128)(2,1)S(1)} %collective-permute-done.4), channel_id=1, source_target_pairs={{0,28},{4,0},{8,4},{12,8},{16,12},{20,16},{24,20},{28,24},{1,29},{... | collective-permute-start | bytes 1056776 | tf_op jit(solution)/shard_map/ppermute | solution.py:25
  136.0 70.9 %collective-permute-start.3 = (bf16[2,128,688]{1,2,0:T(8,128)(2,1)}, bf16[2,128,688]{1,2,0:T(8,128)(2,1)}, u32[]{:S(2)}, u32[]{:S(2)}) collective-permute-start(bf16[2,128,688]{1,2,0:T(8,128)(2,1)} %collective-permute-done.2), channel_id=1, source_target_pairs={{0,4},{4,8},{8,12},{12,16},{16,20},{20,24},{24,28},{28,0},{1,5},{5... | collective-permute-start | bytes 1056776 | tf_op jit(solution)/shard_map/ppermute | solution.py:23
  188.9 6.5 copy-start.15
  188.9 13.4 copy-start.6
  188.9 7.8 copy-start.16
  202.3 10.0 copy-start.10
  202.3 8.3 copy-start.23
  202.3 9.2 copy-start.21
  202.3 383.9 %all-reduce.5.cloned.1.call-start = ((), (), s32[]{:S(2)}) async-start(), calls=%async_computation.12 | async-start | bytes 16777216 | tf_op jit(solution)/shard_map/psum | solution.py:183
  202.4 13.2 collective-permute-start.6
  407.6 12.6 copy-start.43
  433.1 418.0 %all-gather.8.cloned.1.call-start = ((), (), s32[]{:S(2)}) async-start(), calls=%async_computation.18 | async-start | bytes 1310720 | tf_op jit(solution)/shard_map/all_gather | solution.py:218
  598.6 23.2 %copy-start.17 = (bf16[256,1024]{1,0:T(8,128)(2,1)S(1)}, bf16[256,1024]{1,0:T(8,128)(2,1)}, u32[]{:S(2)}) copy-start(bf16[256,1024]{1,0:T(8,128)(2,1)} %all_gather.21) | copy-start | bytes 1572868
  635.5 6.5 copy-start.4
  670.7 6.5 copy-start.4
  705.9 6.5 copy-start.4
  741.0 6.5 copy-start.4
  777.4 25.6 %copy-start.9 = (bf16[32,8,4,1024]{3,1,2,0:T(8,128)(2,1)}, bf16[32,8,4,1024]{3,1,2,0:T(8,128)(2,1)S(1)}, u32[]{:S(2)}) copy-start(bf16[32,8,4,1024]{3,1,2,0:T(8,128)(2,1)S(1)} %copy.128) | copy-start | bytes 6291460
  784.0 120.0 %reduce-scatter.25.cloned.1.call-start = ((), (), s32[]{:S(2)}) async-start(), calls=%async_computation.20 | async-start | bytes 589824
  784.0 19.0 %slice-start = ((s8[8388608]{0:T(1024)(128)(4,1)}), s8[4194304]{0:T(1024)(128)(4,1)S(1)}, s32[]{:S(2)}) async-start(s8[8388608]{0:T(1024)(128)(4,1)} %bitcast.206), calls=%async_computation.21 | async-start | bytes 8388608
  793.7 9.3 slice-start.1
  793.7 9.3 copy-start.32
  793.7 9.3 copy-start.37
  803.0 18.5 %copy-start.39 = (f32[1024]{0:T(1024)S(1)}, f32[1024]{0:T(1024)}, u32[]{:S(2)}) copy-start(f32[1024]{0:T(1024)} %get-tuple-element.368) | copy-start | bytes 12292
  822.6 139.0 %reduce-scatter.21.cloned.1.call-start = ((), (), s32[]{:S(2)}) async-start(), calls=%async_computation.17 | async-start | bytes 3170304 | tf_op jit(solution)/shard_map/reduce_scatter | solution.py:226
  822.6 11.7 copy-start.8
  834.3 193.7 %reduce-scatter.17.cloned.1.call-start = ((), (), s32[]{:S(2)}) async-start(), calls=%async_computation.15 | async-start | bytes 1179648 | tf_op jit(solution)/shard_map/reduce_scatter | solution.py:224
  843.5 250.3 %reduce-scatter.15.cloned.1.call-start = ((), (), s32[]{:S(2)}) async-start(), calls=%async_computation.14 | async-start | bytes 1179648 | tf_op jit(solution)/shard_map/reduce_scatter | solution.py:223
  851.0 314.3 %reduce-scatter.23.cloned.1.call-start = ((), (), s32[]{:S(2)}) async-start(), calls=%async_computation.19 | async-start | bytes 2359296 | tf_op jit(solution)/shard_map/reduce_scatter | solution.py:222
  853.9 423.1 %reduce-scatter.19.cloned.1.call-start = ((), (), s32[]{:S(2)}) async-start(), calls=%async_computation.16 | async-start | bytes 6340608 | tf_op jit(solution)/shard_map/reduce_scatter | solution.py:225
  877.4 474.4 %reduce-scatter.11.cloned.1.call-start = ((), (), s32[]{:S(2)}) async-start(), calls=%async_computation.11 | async-start | bytes 10485760 | tf_op jit(solution)/shard_map/reduce_scatter | solution.py:173
  889.3 536.9 %reduce-scatter.13.cloned.1.call-start = ((), (), s32[]{:S(2)}) async-start(), calls=%async_computation.13 | async-start | bytes 10485760 | tf_op jit(solution)/shard_map/reduce_scatter | solution.py:215
  902.5 428.9 %copy-start.28 = (f32[128,256]{1,0:T(8,128)S(1)}, f32[128,256]{1,0:T(8,128)}, u32[]{:S(2)}) copy-start(f32[128,256]{1,0:T(8,128)} %param.36) | copy-start | bytes 393220
  902.5 432.8 %copy-start.24 = (f32[688,128]{1,0:T(8,128)S(1)}, f32[688,128]{1,0:T(8,128)}, u32[]{:S(2)}) copy-start(f32[688,128]{1,0:T(8,128)} %param.48) | copy-start | bytes 1056772
  902.5 435.3 %copy-start.11 = (f32[2,128,688]{1,2,0:T(8,128)S(1)}, f32[2,128,688]{1,2,0:T(8,128)}, u32[]{:S(2)}) copy-start(f32[2,128,688]{1,2,0:T(8,128)} %param.44) | copy-start | bytes 2113540
  905.1 416.6 %copy-start.40 = (f32[1,128]{1,0:T(1,128)}, f32[1,128]{1,0:T(1,128)S(1)}, u32[]{:S(2)}) copy-start(f32[1,128]{1,0:T(1,128)S(1)} %copy.124) | copy-start | bytes 1540
  911.3 410.5 %copy-start.41 = (f32[1,128]{1,0:T(1,128)}, f32[1,128]{1,0:T(1,128)S(1)}, u32[]{:S(2)}) copy-start(f32[1,128]{1,0:T(1,128)S(1)} %psum.30) | copy-start | bytes 1540
  961.6 373.7 %copy-start.25 = (f32[688,128]{1,0:T(8,128)S(1)}, f32[688,128]{1,0:T(8,128)}, u32[]{:S(2)}) copy-start(f32[688,128]{1,0:T(8,128)} %reduce-scatter.21.cloned.1.call-done) | copy-start | bytes 1056772
  1276.9 60.9 %copy-start.18 = (f32[2,128,688]{1,2,0:T(8,128)S(1)}, f32[2,128,688]{1,2,0:T(8,128)}, u32[]{:S(2)}) copy-start(f32[2,128,688]{1,2,0:T(8,128)} %reduce-scatter.19.cloned.1.call-done) | copy-start | bytes 2113540
  (24 other events, 72.5 us)
Sparse Core Ops, SparseCore 0:
  10.8 47.1 all-gather.3
  60.6 48.7 all-gather.5
  202.4 154.0 all-reduce.2
  433.2 153.0 all-reduce.4
  784.1 16.8 all-gather.7
  822.7 62.0 reduce-scatter.24
  889.3 72.2 reduce-scatter.20
  965.4 62.5 reduce-scatter.16
  1031.4 62.3 reduce-scatter.14
  1098.2 67.0 reduce-scatter.22
  1169.4 107.4 reduce-scatter.18
  1279.6 72.1 reduce-scatter.10
  1354.3 71.7 reduce-scatter.12
